TPU v7x, 32 devices: a whole 2x2x4 slice. The times are simulated.
32 devices in a mesh: tiles: 8 (over z, x), lev: 4 (over y, core).
Axes of the slice: x: 2, y: 2, z: 4, core: 2. Of those that a mesh axis runs over, the one named last changes fastest.
Arguments:
- land_smb: bfloat16 [512, 10, 128], P(('tiles', 'lev')), may hold values from -6 to 6
- block_weights: bfloat16 [1024, 128, 1024], P(('tiles', 'lev')), may hold values from -0.5 to 0.5
- block_tile: int32 [1024], P(('tiles', 'lev')), may hold values from 0 to 255, as said below
- block_land: int32 [1024], P(('tiles', 'lev')), may hold values from 0 to 15
- block_class: int32 [1024], P(('tiles', 'lev')), may hold values from 0 to 9
- ice_mask: int32 [64, 4096], P('tiles', 'lev'), may hold values 0 or 1
- thickness: float32 [64, 4096], P('tiles', 'lev'), may hold values from 0.5 to 2
- prev_smb: float32 [64, 4096], P('tiles', 'lev'), may hold values from -6 to 6
- basal_friction: float32 [64, 4096], P('tiles', 'lev'), may hold values from 0.05 to 0.5
- driving: float32 [10, 64, 4096], P(None, 'tiles', 'lev'), may hold values from -54 to 54
- velocity_start: float32 [10, 64, 4096], P(None, 'tiles', 'lev'), may hold values from -6 to 6
Outputs:
- ice_smb: float32 [64, 4096], P('tiles')
- velocity_end: float32 [10, 64, 4096], P(None, 'tiles', 'lev')
Inputs may be any that keep to these rules, and one draw needn't show every extreme that they name: `block_tile`: ice tile t lies on index t // 32 of tiles. Of the 32 remap blocks of one device, at most 8 name tiles on any one index of tiles; in every draw some index of tiles receives exactly 8 from every device.
All inputs are finite; a program needn't handle non-finite values. No bound on the sum of `ice_mask` on one device may be relied on, other than what follows from the above.
Results may differ from a plain program's by a relative error of at most 0.0003.
Values sent between devices are 32-bit elements; how exact they have to be, the bound alone decides.
A program may use at most 64 MiB of HBM per device.

v0:
```python
import jax
import jax.numpy as jnp
from jax import lax
from jax.sharding import PartitionSpec as P

CX = 8
TW = 128
TPD = 32
ITERS = 4
VISC_FLOOR = 0.25
VERTICAL = 4.0
SMB_WEIGHT = 0.5


def extended(cells, sides, width):
    for axis, dim in sides:
        count = lax.axis_size(axis)
        ends = count - 1
        head = lax.slice_in_dim(cells, 0, width, axis=dim)
        tail = lax.slice_in_dim(cells, cells.shape[dim] - width, cells.shape[dim], axis=dim)
        cells = jnp.concatenate(
            [
                lax.ppermute(tail, axis, [(i, (i + 1) % count) for i in range(ends)]),
                cells,
                lax.ppermute(head, axis, [((i + 1) % count, i) for i in range(ends)]),
            ],
            axis=dim,
        )
    return cells


def visc_from(box, ice_frac):
    slope_x = (box[:, 2:, 1:-1] - box[:, :-2, 1:-1]) * 0.5
    slope_y = (box[:, 1:-1, 2:] - box[:, 1:-1, :-2]) * 0.5
    return ice_frac * (VISC_FLOOR + slope_x * slope_x + slope_y * slope_y) ** (-1.0 / 3.0)


def level_pad(box):
    return jnp.pad(box, ((1, 1), (0, 0), (0, 0)))


def face_weights(visc_box, drag):
    center = visc_box[1:-1, 1:-1, 1:-1]
    east_face = jnp.sqrt(center * visc_box[1:-1, 2:, 1:-1])
    west_face = jnp.sqrt(center * visc_box[1:-1, :-2, 1:-1])
    north_face = jnp.sqrt(center * visc_box[1:-1, 1:-1, 2:])
    south_face = jnp.sqrt(center * visc_box[1:-1, 1:-1, :-2])
    upper_face = VERTICAL * jnp.sqrt(center * visc_box[2:, 1:-1, 1:-1])
    lower_face = VERTICAL * jnp.sqrt(center * visc_box[:-2, 1:-1, 1:-1])
    diagonal_sum = drag + east_face + west_face + north_face + south_face + upper_face + lower_face
    return (diagonal_sum, east_face, west_face, upper_face, lower_face, north_face, south_face)


def apply_operator(faces, field_box):
    diagonal_sum, east_face, west_face, upper_face, lower_face, north_face, south_face = faces
    center = field_box[1:-1, 1:-1, 1:-1]
    result = (
        diagonal_sum * center
        - east_face * field_box[1:-1, 2:, 1:-1]
        - west_face * field_box[1:-1, :-2, 1:-1]
    )
    result = (
        result - upper_face * field_box[2:, 1:-1, 1:-1] - lower_face * field_box[:-2, 1:-1, 1:-1]
    )
    return result - north_face * field_box[1:-1, 1:-1, 2:] - south_face * field_box[1:-1, 1:-1, :-2]


def apply_local(faces, field):
    field_box = extended(field, (("tiles", 1), ("lev", 2)), 1)
    return apply_operator(faces, level_pad(field_box))


def paired_totals(residual, image):
    return lax.psum((jnp.sum(residual * residual), jnp.sum(residual * image)), ("tiles", "lev"))


def krylov_merged(faces, rhs, start):
    solution = start
    residual = rhs - apply_local(faces, start)
    image = apply_local(faces, residual)
    norm_now, product = paired_totals(residual, image)
    step_len = norm_now / product
    direction = residual
    along = image
    for iteration in range(ITERS):
        solution = solution + step_len * direction
        residual = residual - step_len * along
        if iteration + 1 < ITERS:
            image = apply_local(faces, residual)
            norm_next, product = paired_totals(residual, image)
            ratio = norm_next / norm_now
            step_len = norm_next / (product - ratio * norm_next / step_len)
            direction = residual + ratio * direction
            along = image + ratio * along
            norm_now = norm_next
    return solution


def sent_visc(velocity, ice_frac):
    x_box = extended(velocity, (("tiles", 1), ("lev", 2)), 1)
    viscosity = visc_from(x_box, ice_frac)
    visc_box = extended(viscosity, (("tiles", 1), ("lev", 2)), 1)
    return level_pad(visc_box)


def body(
    land_smb,
    block_weights,
    block_tile,
    block_land,
    block_class,
    ice_mask,
    thickness,
    prev_smb,
    basal_friction,
    driving,
    velocity_start,
):
    local_blocks, classes, land_cols = land_smb.shape
    blocks_here = block_tile.shape[0]
    tile_cells = block_weights.shape[2]
    land_rows = land_smb.reshape(local_blocks * classes, land_cols)
    picked = land_rows[block_land * classes + block_class]
    products = jnp.einsum("bl,blt->bt", picked, block_weights, preferred_element_type=jnp.float32)
    owners = lax.axis_size("tiles")
    capacity = max(2, 2 * blocks_here // owners)
    destination = block_tile // TPD
    local_tile = block_tile % TPD
    positions = jnp.arange(blocks_here, dtype=jnp.int32)
    earlier = jnp.logical_and(
        destination[None, :] == destination[:, None], positions[None, :] < positions[:, None]
    )
    ranks = jnp.sum(earlier.astype(jnp.int32), axis=1)
    slots = destination * capacity + ranks
    slot_ids = jnp.arange(owners * capacity, dtype=jnp.int32)
    slot_match = slots[None, :] == slot_ids[:, None]
    slot_hot = slot_match.astype(jnp.float32)
    sending = jnp.dot(
        slot_hot, products, precision=lax.Precision.HIGHEST, preferred_element_type=jnp.float32
    )
    sending = sending.reshape(owners, capacity, tile_cells)
    slot_tile = jnp.sum(jnp.where(slot_match, (local_tile + 1)[None, :], 0), axis=1) - 1
    slot_tile = slot_tile.reshape(owners, capacity)
    received, recv_tile = (
        lax.all_to_all(sending, "tiles", split_axis=0, concat_axis=0, tiled=True),
        lax.all_to_all(slot_tile, "tiles", split_axis=0, concat_axis=0, tiled=True),
    )
    tile_hot = (recv_tile.reshape(-1)[None, :] == jnp.arange(TPD, dtype=jnp.int32)[:, None]).astype(
        jnp.float32
    )
    partial_sums = jnp.dot(
        tile_hot,
        received.reshape(-1, tile_cells),
        precision=lax.Precision.HIGHEST,
        preferred_element_type=jnp.float32,
    )
    totals = lax.psum(partial_sums, "lev")
    ice_smb = totals.reshape(TPD, CX, TW).transpose(1, 0, 2).reshape(CX, TPD * TW)
    ice_frac = ice_mask.astype(jnp.float32)
    rhs = (ice_frac * (thickness + SMB_WEIGHT * prev_smb))[None] * driving
    drag = (ice_frac * basal_friction + (1.0 - ice_frac))[None]
    velocity = velocity_start
    visc_box = sent_visc(velocity, ice_frac[None])
    faces = face_weights(visc_box, drag)
    velocity = krylov_merged(faces, rhs, velocity)
    return (ice_smb, velocity)


def solution(mesh):
    in_specs = (
        P(("tiles", "lev"), None, None),
        P(("tiles", "lev"), None, None),
        P(("tiles", "lev")),
        P(("tiles", "lev")),
        P(("tiles", "lev")),
        P("tiles", "lev"),
        P("tiles", "lev"),
        P("tiles", "lev"),
        P("tiles", "lev"),
        P(None, "tiles", "lev"),
        P(None, "tiles", "lev"),
    )
    out_specs = (P("tiles", None), P(None, "tiles", "lev"))
    return jax.shard_map(body, mesh=mesh, in_specs=in_specs, out_specs=out_specs, check_vma=False)
```

profile of v0, /device:TPU:0, one launch (start us, length us, event | category | flops | bytes accessed | tf_op | source)
XLA Modules:
  0.0 379.7 jit_solution(6685467221838924000)
XLA Ops:
  8.3 1.3 collective-permute-start
  9.6 5.5 %collective-permute-start.1 = (f32[10,1,1024]{2,1,0:T(1,128)S(1)}, f32[10,1,1024]{2,1,0:T(1,128)S(1)}, u32[]{:S(2)}, u32[]{:S(2)}) collective-permute-start(f32[10,1,1024]{2,1,0:T(1,128)S(1)} %get-tuple-element.46), channel_id=1, source_target_pairs={{0,4},{4,8},{8,12},{12,16},{16,20},{20,24},{24,28},{1,5},{5,9},{9,... | collective-permute-start | bytes 122888 | tf_op jit(solution)/shard_map/ppermute | solution.py:23
  15.2 1.6 collective-permute-done.1
  18.0 1.3 collective-permute-start.2
  19.3 3.0 collective-permute-start.3
  22.3 1.4 add_multiply_fusion
  24.5 2.2 power_multiply_fusion
  26.8 1.3 collective-permute-start.4
  28.1 5.4 %collective-permute-start.5 = (f32[10,1,1024]{2,1,0:T(1,128)S(1)}, f32[10,1,1024]{2,1,0:T(1,128)S(1)}, u32[]{:S(2)}, u32[]{:S(2)}) collective-permute-start(f32[10,1,1024]{2,1,0:T(1,128)S(1)} %get-tuple-element.44), channel_id=1, source_target_pairs={{0,4},{4,8},{8,12},{12,16},{16,20},{20,24},{24,28},{1,5},{5,9},{9,... | collective-permute-start | bytes 122888 | tf_op jit(solution)/shard_map/ppermute | solution.py:23
  35.9 1.3 collective-permute-start.6
  37.2 3.0 collective-permute-start.7
  42.0 3.4 fusion.11
  45.5 1.3 collective-permute-start.8
  46.8 5.4 %collective-permute-start.9 = (f32[10,1,1024]{2,1,0:T(1,128)S(1)}, f32[10,1,1024]{2,1,0:T(1,128)S(1)}, u32[]{:S(2)}, u32[]{:S(2)}) collective-permute-start(f32[10,1,1024]{2,1,0:T(1,128)S(1)} %get-tuple-element.42), channel_id=1, source_target_pairs={{0,4},{4,8},{8,12},{12,16},{16,20},{20,24},{24,28},{1,5},{5,9},{9,... | collective-permute-start | bytes 122888 | tf_op jit(solution)/shard_map/ppermute | solution.py:23
  54.1 3.5 collective-permute-start.10
  57.6 1.3 collective-permute-start.11
  59.6 3.9 %collective-permute-done.11 = f32[10,10,1]{2,1,0:T(8,128)S(1)} collective-permute-done((f32[10,10,1]{2,1,0:T(8,128)S(1)}, f32[10,10,1]{2,1,0:T(8,128)S(1)}, u32[]{:S(2)}, u32[]{:S(2)}) %collective-permute-start.11) | collective-permute-done | bytes 432 | tf_op jit(solution)/shard_map/ppermute | solution.py:25
  64.6 3.3 multiply_reduce_fusion.5
  67.9 45.4 %all-reduce.9 = (f32[]{:T(128)}, f32[]{:T(128)}) all-reduce(f32[]{:T(128)} %get-tuple-element.7, f32[]{:T(128)} %get-tuple-element.6), channel_id=1, replica_groups=mesh['tiles'=8,'lev'=4] {'tiles','lev'}, use_global_device_ids=true, to_apply=%region_4.5 | all-reduce | flops 2 | bytes 16 | tf_op jit(solution)/shard_map/psum | solution.py:74
  114.6 1.3 collective-permute-start.12
  115.9 4.8 %collective-permute-start.13 = (f32[10,1,1024]{2,1,0:T(1,128)S(1)}, f32[10,1,1024]{2,1,0:T(1,128)S(1)}, u32[]{:S(2)}, u32[]{:S(2)}) collective-permute-start(f32[10,1,1024]{2,1,0:T(1,128)S(1)} %get-tuple-element.40), channel_id=1, source_target_pairs={{0,4},{4,8},{8,12},{12,16},{16,20},{20,24},{24,28},{1,5},{5,9},{9,... | collective-permute-start | bytes 122888 | tf_op jit(solution)/shard_map/ppermute | solution.py:23
  121.4 5.9 %all-to-all-start = ((s32[8,1,8]{2,1,0:T(1,128)}), s32[8,1,8]{2,1,0:T(1,128)}, u32[]{:S(2)}, u32[]{:S(2)}) async-start(s32[8,1,8]{2,1,0:T(1,128)} %bitcast), calls=%async_computation | async-start | bytes 8192 | tf_op jit(solution)/shard_map/all_to_all | solution.py:146
  127.6 1.3 collective-permute-start.14
  128.9 1.3 collective-permute-start.15
  131.4 3.0 collective-permute-done.15
  135.6 3.3 multiply_reduce_fusion.3
  138.8 42.6 %all-reduce.8 = (f32[]{:T(128)}, f32[]{:T(128)}) all-reduce(f32[]{:T(128)} %get-tuple-element.5, f32[]{:T(128)} %get-tuple-element.4), channel_id=1, replica_groups=mesh['tiles'=8,'lev'=4] {'tiles','lev'}, use_global_device_ids=true, to_apply=%region_8.9 | all-reduce | flops 2 | bytes 16 | tf_op jit(solution)/shard_map/psum | solution.py:74
  186.2 1.3 collective-permute-start.16
  187.5 4.8 %collective-permute-start.17 = (f32[10,1,1024]{2,1,0:T(1,128)S(1)}, f32[10,1,1024]{2,1,0:T(1,128)S(1)}, u32[]{:S(2)}, u32[]{:S(2)}) collective-permute-start(f32[10,1,1024]{2,1,0:T(1,128)S(1)} %get-tuple-element.38), channel_id=1, source_target_pairs={{0,4},{4,8},{8,12},{12,16},{16,20},{20,24},{24,28},{1,5},{5,9},{9,... | collective-permute-start | bytes 122888 | tf_op jit(solution)/shard_map/ppermute | solution.py:23
  196.5 1.3 collective-permute-start.18
  197.8 1.5 collective-permute-start.19
  199.2 5.2 %fusion.74 = f32[32,1,1024]{2,1,0:T(1,128)} fusion(bf16[32,128,1024]{2,1,0:T(8,128)(2,1)} %param.12, bf16[32,128,1]{1,0,2:T(8,128)(2,1)S(1)} %bitcast.19), kind=kOutput, calls=%fused_computation.159 | convolution fusion | flops 8388608 | bytes 8527872 | tf_op jit(solution)/shard_map/bl,blt->bt/dot_general | solution.py:124
  204.5 2.3 concatenate.141
  206.8 4.0 %multiply_reduce_fusion.1 = (f32[]{:T(128)}, f32[]{:T(128)}, f32[10,8,1024]{2,1,0:T(8,128)}) fusion(f32[10,8,1024]{2,1,0:T(8,128)S(1)} %multiply_subtract_fusion.1, f32[10,1,1024]{2,1,0:T(1,128)S(1)} %collective-permute-done.16, f32[10,1,1024]{2,1,0:T(1,128)S(1)} %collective-permute-done.17, f32[10,10,1]{2,1,0:T(8,128)S(1)} %collective-permute-done.18, ...), kind=kLoop, calls=%fused_computation.142 | loop fusion | flops 3522558 | bytes 2247016 | tf_op jit(solution)/shard_map/reduce_sum | solution.py:74
  210.8 44.5 %all-reduce.7 = (f32[]{:T(128)}, f32[]{:T(128)}) all-reduce(f32[]{:T(128)} %get-tuple-element.3, f32[]{:T(128)} %get-tuple-element.2), channel_id=1, replica_groups=mesh['tiles'=8,'lev'=4] {'tiles','lev'}, use_global_device_ids=true, to_apply=%region_12.13 | all-reduce | flops 2 | bytes 16 | tf_op jit(solution)/shard_map/psum | solution.py:74
  259.1 1.8 multiply_reduce_fusion
  260.9 1.3 collective-permute-start.20
  262.2 4.8 %collective-permute-start.21 = (f32[10,1,1024]{2,1,0:T(1,128)S(1)}, f32[10,1,1024]{2,1,0:T(1,128)S(1)}, u32[]{:S(2)}, u32[]{:S(2)}) collective-permute-start(f32[10,1,1024]{2,1,0:T(1,128)S(1)} %get-tuple-element.36), channel_id=1, source_target_pairs={{0,4},{4,8},{8,12},{12,16},{16,20},{20,24},{24,28},{1,5},{5,9},{9,... | collective-permute-start | bytes 122888 | tf_op jit(solution)/shard_map/ppermute | solution.py:23
  267.0 2.0 convolution_bitcast_fusion
  270.3 6.3 %all-to-all-start.1 = ((f32[8,8,1024]{2,1,0:T(8,128)}), f32[8,8,1024]{2,1,0:T(8,128)}, u32[]{:S(2)}, u32[]{:S(2)}) async-start(f32[8,8,1024]{2,1,0:T(8,128)} %convolution_bitcast_fusion), calls=%async_computation.1 | async-start | bytes 524288 | tf_op jit(solution)/shard_map/all_to_all | solution.py:145
  277.4 1.9 collective-permute-start.22
  281.1 1.9 reduce.3
  283.0 1.3 eq.49
  284.7 2.1 concatenate.147
  286.8 3.4 fusion.70
  290.2 43.7 %all-reduce.6 = (f32[]{:T(128)}, f32[]{:T(128)}) all-reduce(f32[]{:T(128)} %get-tuple-element.16, f32[]{:T(128)} %fusion.70), channel_id=1, replica_groups=mesh['tiles'=8,'lev'=4] {'tiles','lev'}, use_global_device_ids=true, to_apply=%region_16.17 | all-reduce | flops 2 | bytes 16 | tf_op jit(solution)/shard_map/psum | solution.py:74
  340.2 31.1 %all-reduce.12.cloned.1.call-done = f32[8,4096]{1,0:T(8,128)} async-done(((f32[8,4096]{1,0:T(8,128)}), f32[8,4096]{1,0:T(8,128)}) %all-reduce.12.cloned.1.call-update) | async-done | bytes 131088 | tf_op jit(solution)/shard_map/psum | solution.py:157
  371.3 1.6 copy.29
  (96 shorter events, 25.6 us)
Async XLA Ops:
  8.3 6.8 %collective-permute-start = (f32[10,1,1024]{2,1,0:T(1,128)S(1)}, f32[10,1,1024]{2,1,0:T(1,128)S(1)}, u32[]{:S(2)}, u32[]{:S(2)}) collective-permute-start(f32[10,1,1024]{2,1,0:T(1,128)S(1)} %get-tuple-element.47), channel_id=1, source_target_pairs={{4,0},{8,4},{12,8},{16,12},{20,16},{24,20},{28,24},{5,1},{9,5},{13... | collective-permute-start | bytes 122888 | tf_op jit(solution)/shard_map/ppermute | solution.py:25
  9.6 7.2 %collective-permute-start.1 = (f32[10,1,1024]{2,1,0:T(1,128)S(1)}, f32[10,1,1024]{2,1,0:T(1,128)S(1)}, u32[]{:S(2)}, u32[]{:S(2)}) collective-permute-start(f32[10,1,1024]{2,1,0:T(1,128)S(1)} %get-tuple-element.46), channel_id=1, source_target_pairs={{0,4},{4,8},{8,12},{12,16},{16,20},{20,24},{24,28},{1,5},{5,9},{9,... | collective-permute-start | bytes 122888 | tf_op jit(solution)/shard_map/ppermute | solution.py:23
  15.1 19.6 %copy-start.9 = (f32[10,1,1024]{2,1,0:T(1,128)}, f32[10,1,1024]{2,1,0:T(1,128)S(1)}, u32[]{:S(2)}) copy-start(f32[10,1,1024]{2,1,0:T(1,128)S(1)} %collective-permute-done) | copy-start | bytes 122884
  16.8 18.0 %copy-start.10 = (f32[10,1,1024]{2,1,0:T(1,128)}, f32[10,1,1024]{2,1,0:T(1,128)S(1)}, u32[]{:S(2)}) copy-start(f32[10,1,1024]{2,1,0:T(1,128)S(1)} %collective-permute-done.1) | copy-start | bytes 122884
  18.0 6.5 %collective-permute-start.2 = (f32[10,10,1]{2,1,0:T(8,128)S(1)}, f32[10,10,1]{2,1,0:T(8,128)S(1)}, u32[]{:S(2)}, u32[]{:S(2)}) collective-permute-start(f32[10,10,1]{2,1,0:T(8,128)S(1)} %get-tuple-element.34), channel_id=1, source_target_pairs={{1,0},{2,1},{3,2},{5,4},{6,5},{7,6},{9,8},{10,9},{11,10},{13,12},{... | collective-permute-start | bytes 1208 | tf_op jit(solution)/shard_map/ppermute | solution.py:25
  19.3 5.2 %collective-permute-start.3 = (f32[10,10,1]{2,1,0:T(8,128)S(1)}, f32[10,10,1]{2,1,0:T(8,128)S(1)}, u32[]{:S(2)}, u32[]{:S(2)}) collective-permute-start(f32[10,10,1]{2,1,0:T(8,128)S(1)} %get-tuple-element.35), channel_id=1, source_target_pairs={{0,1},{1,2},{2,3},{4,5},{5,6},{6,7},{8,9},{9,10},{10,11},{12,13},{... | collective-permute-start | bytes 1208 | tf_op jit(solution)/shard_map/ppermute | solution.py:23
  24.5 17.3 %copy-start.7 = (f32[10,10,1]{2,1,0:T(8,128)}, f32[10,10,1]{2,1,0:T(8,128)S(1)}, u32[]{:S(2)}) copy-start(f32[10,10,1]{2,1,0:T(8,128)S(1)} %collective-permute-done.2) | copy-start | bytes 1204
  24.5 17.3 %copy-start.8 = (f32[10,10,1]{2,1,0:T(8,128)}, f32[10,10,1]{2,1,0:T(8,128)S(1)}, u32[]{:S(2)}) copy-start(f32[10,10,1]{2,1,0:T(8,128)S(1)} %collective-permute-done.3) | copy-start | bytes 1204
  26.8 7.9 %collective-permute-start.4 = (f32[10,1,1024]{2,1,0:T(1,128)S(1)}, f32[10,1,1024]{2,1,0:T(1,128)S(1)}, u32[]{:S(2)}, u32[]{:S(2)}) collective-permute-start(f32[10,1,1024]{2,1,0:T(1,128)S(1)} %get-tuple-element.45), channel_id=1, source_target_pairs={{4,0},{8,4},{12,8},{16,12},{20,16},{24,20},{28,24},{5,1},{9,5},{13... | collective-permute-start | bytes 122888 | tf_op jit(solution)/shard_map/ppermute | solution.py:25
  28.1 7.6 %collective-permute-start.5 = (f32[10,1,1024]{2,1,0:T(1,128)S(1)}, f32[10,1,1024]{2,1,0:T(1,128)S(1)}, u32[]{:S(2)}, u32[]{:S(2)}) collective-permute-start(f32[10,1,1024]{2,1,0:T(1,128)S(1)} %get-tuple-element.44), channel_id=1, source_target_pairs={{0,4},{4,8},{8,12},{12,16},{16,20},{20,24},{24,28},{1,5},{5,9},{9,... | collective-permute-start | bytes 122888 | tf_op jit(solution)/shard_map/ppermute | solution.py:23
  34.7 6.6 %copy-start.14 = (s32[32]{0:T(128)}, s32[32]{0:T(128)S(1)}, u32[]{:S(2)}) copy-start(s32[32]{0:T(128)S(1)} %get-tuple-element.51) | copy-start | bytes 388
  34.7 5.5 %copy-start.3 = (f32[10,1,1024]{2,1,0:T(1,128)}, f32[10,1,1024]{2,1,0:T(1,128)S(1)}, u32[]{:S(2)}) copy-start(f32[10,1,1024]{2,1,0:T(1,128)S(1)} %collective-permute-done.4) | copy-start | bytes 122884
  35.6 4.6 %copy-start.5 = (f32[10,1,1024]{2,1,0:T(1,128)}, f32[10,1,1024]{2,1,0:T(1,128)S(1)}, u32[]{:S(2)}) copy-start(f32[10,1,1024]{2,1,0:T(1,128)S(1)} %collective-permute-done.5) | copy-start | bytes 122884
  35.9 5.5 %collective-permute-start.6 = (f32[10,10,1]{2,1,0:T(8,128)S(1)}, f32[10,10,1]{2,1,0:T(8,128)S(1)}, u32[]{:S(2)}, u32[]{:S(2)}) collective-permute-start(f32[10,10,1]{2,1,0:T(8,128)S(1)} %get-tuple-element.33), channel_id=1, source_target_pairs={{1,0},{2,1},{3,2},{5,4},{6,5},{7,6},{9,8},{10,9},{11,10},{13,12},{... | collective-permute-start | bytes 1208 | tf_op jit(solution)/shard_map/ppermute | solution.py:25
  37.2 4.2 %collective-permute-start.7 = (f32[10,10,1]{2,1,0:T(8,128)S(1)}, f32[10,10,1]{2,1,0:T(8,128)S(1)}, u32[]{:S(2)}, u32[]{:S(2)}) collective-permute-start(f32[10,10,1]{2,1,0:T(8,128)S(1)} %get-tuple-element.32), channel_id=1, source_target_pairs={{0,1},{1,2},{2,3},{4,5},{5,6},{6,7},{8,9},{9,10},{10,11},{12,13},{... | collective-permute-start | bytes 1208 | tf_op jit(solution)/shard_map/ppermute | solution.py:23
  41.4 0.6 copy-start.1
  45.4 90.2 %copy-start.2 = (f32[10,10,1]{2,1,0:T(8,128)S(1)}, f32[10,10,1]{2,1,0:T(8,128)}, u32[]{:S(2)}) copy-start(f32[10,10,1]{2,1,0:T(8,128)} %copy-done.1) | copy-start | bytes 1204
  45.4 90.2 %copy-start.4 = (f32[10,1,1024]{2,1,0:T(1,128)S(1)}, f32[10,1,1024]{2,1,0:T(1,128)}, u32[]{:S(2)}) copy-start(f32[10,1,1024]{2,1,0:T(1,128)} %copy-done.3) | copy-start | bytes 122884
  45.4 90.2 %copy-start.6 = (f32[10,1,1024]{2,1,0:T(1,128)S(1)}, f32[10,1,1024]{2,1,0:T(1,128)}, u32[]{:S(2)}) copy-start(f32[10,1,1024]{2,1,0:T(1,128)} %copy-done.5) | copy-start | bytes 122884
  45.5 7.4 %collective-permute-start.8 = (f32[10,1,1024]{2,1,0:T(1,128)S(1)}, f32[10,1,1024]{2,1,0:T(1,128)S(1)}, u32[]{:S(2)}, u32[]{:S(2)}) collective-permute-start(f32[10,1,1024]{2,1,0:T(1,128)S(1)} %get-tuple-element.43), channel_id=1, source_target_pairs={{4,0},{8,4},{12,8},{16,12},{20,16},{24,20},{28,24},{5,1},{9,5},{13... | collective-permute-start | bytes 122888 | tf_op jit(solution)/shard_map/ppermute | solution.py:25
  46.8 7.1 %collective-permute-start.9 = (f32[10,1,1024]{2,1,0:T(1,128)S(1)}, f32[10,1,1024]{2,1,0:T(1,128)S(1)}, u32[]{:S(2)}, u32[]{:S(2)}) collective-permute-start(f32[10,1,1024]{2,1,0:T(1,128)S(1)} %get-tuple-element.42), channel_id=1, source_target_pairs={{0,4},{4,8},{8,12},{12,16},{16,20},{20,24},{24,28},{1,5},{5,9},{9,... | collective-permute-start | bytes 122888 | tf_op jit(solution)/shard_map/ppermute | solution.py:23
  52.9 74.5 %copy-start.13 = (s32[32]{0:T(128)}, s32[32]{0:T(128)S(1)}, u32[]{:S(2)}) copy-start(s32[32]{0:T(128)S(1)} %multiply_add_fusion.2) | copy-start | bytes 388
  54.1 5.5 %collective-permute-start.10 = (f32[10,10,1]{2,1,0:T(8,128)S(1)}, f32[10,10,1]{2,1,0:T(8,128)S(1)}, u32[]{:S(2)}, u32[]{:S(2)}) collective-permute-start(f32[10,10,1]{2,1,0:T(8,128)S(1)} %get-tuple-element.31), channel_id=1, source_target_pairs={{0,1},{1,2},{2,3},{4,5},{5,6},{6,7},{8,9},{9,10},{10,11},{12,13},{... | collective-permute-start | bytes 1208 | tf_op jit(solution)/shard_map/ppermute | solution.py:23
  57.6 5.9 %collective-permute-start.11 = (f32[10,10,1]{2,1,0:T(8,128)S(1)}, f32[10,10,1]{2,1,0:T(8,128)S(1)}, u32[]{:S(2)}, u32[]{:S(2)}) collective-permute-start(f32[10,10,1]{2,1,0:T(8,128)S(1)} %get-tuple-element.30), channel_id=1, source_target_pairs={{1,0},{2,1},{3,2},{5,4},{6,5},{7,6},{9,8},{10,9},{11,10},{13,12},{... | collective-permute-start | bytes 1208 | tf_op jit(solution)/shard_map/ppermute | solution.py:25
  114.6 12.7 %collective-permute-start.12 = (f32[10,1,1024]{2,1,0:T(1,128)S(1)}, f32[10,1,1024]{2,1,0:T(1,128)S(1)}, u32[]{:S(2)}, u32[]{:S(2)}) collective-permute-start(f32[10,1,1024]{2,1,0:T(1,128)S(1)} %get-tuple-element.41), channel_id=1, source_target_pairs={{4,0},{8,4},{12,8},{16,12},{20,16},{24,20},{28,24},{5,1},{9,5},{13... | collective-permute-start | bytes 122888 | tf_op jit(solution)/shard_map/ppermute | solution.py:25
  115.9 11.4 %collective-permute-start.13 = (f32[10,1,1024]{2,1,0:T(1,128)S(1)}, f32[10,1,1024]{2,1,0:T(1,128)S(1)}, u32[]{:S(2)}, u32[]{:S(2)}) collective-permute-start(f32[10,1,1024]{2,1,0:T(1,128)S(1)} %get-tuple-element.40), channel_id=1, source_target_pairs={{0,4},{4,8},{8,12},{12,16},{16,20},{20,24},{24,28},{1,5},{5,9},{9,... | collective-permute-start | bytes 122888 | tf_op jit(solution)/shard_map/ppermute | solution.py:23
  121.4 148.9 %all-to-all-start = ((s32[8,1,8]{2,1,0:T(1,128)}), s32[8,1,8]{2,1,0:T(1,128)}, u32[]{:S(2)}, u32[]{:S(2)}) async-start(s32[8,1,8]{2,1,0:T(1,128)} %bitcast), calls=%async_computation | async-start | bytes 8192 | tf_op jit(solution)/shard_map/all_to_all | solution.py:146
  127.6 3.8 collective-permute-start.14
  128.9 5.5 %collective-permute-start.15 = (f32[10,10,1]{2,1,0:T(8,128)S(1)}, f32[10,10,1]{2,1,0:T(8,128)S(1)}, u32[]{:S(2)}, u32[]{:S(2)}) collective-permute-start(f32[10,10,1]{2,1,0:T(8,128)S(1)} %get-tuple-element.28), channel_id=1, source_target_pairs={{1,0},{2,1},{3,2},{5,4},{6,5},{7,6},{9,8},{10,9},{11,10},{13,12},{... | collective-permute-start | bytes 1208 | tf_op jit(solution)/shard_map/ppermute | solution.py:25
  186.2 8.2 %collective-permute-start.16 = (f32[10,1,1024]{2,1,0:T(1,128)S(1)}, f32[10,1,1024]{2,1,0:T(1,128)S(1)}, u32[]{:S(2)}, u32[]{:S(2)}) collective-permute-start(f32[10,1,1024]{2,1,0:T(1,128)S(1)} %get-tuple-element.39), channel_id=1, source_target_pairs={{4,0},{8,4},{12,8},{16,12},{20,16},{24,20},{28,24},{5,1},{9,5},{13... | collective-permute-start | bytes 122888 | tf_op jit(solution)/shard_map/ppermute | solution.py:25
  187.5 6.9 %collective-permute-start.17 = (f32[10,1,1024]{2,1,0:T(1,128)S(1)}, f32[10,1,1024]{2,1,0:T(1,128)S(1)}, u32[]{:S(2)}, u32[]{:S(2)}) collective-permute-start(f32[10,1,1024]{2,1,0:T(1,128)S(1)} %get-tuple-element.38), channel_id=1, source_target_pairs={{0,4},{4,8},{8,12},{12,16},{16,20},{20,24},{24,28},{1,5},{5,9},{9,... | collective-permute-start | bytes 122888 | tf_op jit(solution)/shard_map/ppermute | solution.py:23
  196.5 8.0 %collective-permute-start.18 = (f32[10,10,1]{2,1,0:T(8,128)S(1)}, f32[10,10,1]{2,1,0:T(8,128)S(1)}, u32[]{:S(2)}, u32[]{:S(2)}) collective-permute-start(f32[10,10,1]{2,1,0:T(8,128)S(1)} %get-tuple-element.27), channel_id=1, source_target_pairs={{0,1},{1,2},{2,3},{4,5},{5,6},{6,7},{8,9},{9,10},{10,11},{12,13},{... | collective-permute-start | bytes 1208 | tf_op jit(solution)/shard_map/ppermute | solution.py:23
  197.8 6.7 %collective-permute-start.19 = (f32[10,10,1]{2,1,0:T(8,128)S(1)}, f32[10,10,1]{2,1,0:T(8,128)S(1)}, u32[]{:S(2)}, u32[]{:S(2)}) collective-permute-start(f32[10,10,1]{2,1,0:T(8,128)S(1)} %get-tuple-element.26), channel_id=1, source_target_pairs={{1,0},{2,1},{3,2},{5,4},{6,5},{7,6},{9,8},{10,9},{11,10},{13,12},{... | collective-permute-start | bytes 1208 | tf_op jit(solution)/shard_map/ppermute | solution.py:25
  204.5 134.8 %copy-start = (f32[10,8,1024]{2,1,0:T(8,128)S(1)}, f32[10,8,1024]{2,1,0:T(8,128)}, u32[]{:S(2)}) copy-start(f32[10,8,1024]{2,1,0:T(8,128)} %param.21) | copy-start | bytes 983044
  260.9 8.1 %collective-permute-start.20 = (f32[10,1,1024]{2,1,0:T(1,128)S(1)}, f32[10,1,1024]{2,1,0:T(1,128)S(1)}, u32[]{:S(2)}, u32[]{:S(2)}) collective-permute-start(f32[10,1,1024]{2,1,0:T(1,128)S(1)} %get-tuple-element.37), channel_id=1, source_target_pairs={{4,0},{8,4},{12,8},{16,12},{20,16},{24,20},{28,24},{5,1},{9,5},{13... | collective-permute-start | bytes 122888 | tf_op jit(solution)/shard_map/ppermute | solution.py:25
  262.2 6.8 %collective-permute-start.21 = (f32[10,1,1024]{2,1,0:T(1,128)S(1)}, f32[10,1,1024]{2,1,0:T(1,128)S(1)}, u32[]{:S(2)}, u32[]{:S(2)}) collective-permute-start(f32[10,1,1024]{2,1,0:T(1,128)S(1)} %get-tuple-element.36), channel_id=1, source_target_pairs={{0,4},{4,8},{8,12},{12,16},{16,20},{20,24},{24,28},{1,5},{5,9},{9,... | collective-permute-start | bytes 122888 | tf_op jit(solution)/shard_map/ppermute | solution.py:23
  269.0 0.6 copy-start.11
  269.6 0.6 copy-start.12
  270.3 67.1 %all-to-all-start.1 = ((f32[8,8,1024]{2,1,0:T(8,128)}), f32[8,8,1024]{2,1,0:T(8,128)}, u32[]{:S(2)}, u32[]{:S(2)}) async-start(f32[8,8,1024]{2,1,0:T(8,128)} %convolution_bitcast_fusion), calls=%async_computation.1 | async-start | bytes 524288 | tf_op jit(solution)/shard_map/all_to_all | solution.py:145
  276.6 94.7 %all-reduce.12.cloned.1.call-start = ((), (), s32[]{:S(2)}) async-start(), calls=%async_computation.2 | async-start | bytes 262144 | tf_op jit(solution)/shard_map/psum | solution.py:157
  277.4 6.9 %collective-permute-start.22 = (f32[10,10,1]{2,1,0:T(8,128)}, f32[10,10,1]{2,1,0:T(8,128)}, u32[]{:S(2)}, u32[]{:S(2)}) collective-permute-start(f32[10,10,1]{2,1,0:T(8,128)} %get-tuple-element.25), channel_id=1, source_target_pairs={{0,1},{1,2},{2,3},{4,5},{5,6},{6,7},{8,9},{9,10},{10,11},{12,13},{... | collective-permute-start | bytes 1208 | tf_op jit(solution)/shard_map/ppermute | solution.py:23
  279.3 5.4 %collective-permute-start.23 = (f32[10,10,1]{2,1,0:T(8,128)}, f32[10,10,1]{2,1,0:T(8,128)}, u32[]{:S(2)}, u32[]{:S(2)}) collective-permute-start(f32[10,10,1]{2,1,0:T(8,128)} %get-tuple-element.24), channel_id=1, source_target_pairs={{1,0},{2,1},{3,2},{5,4},{6,5},{7,6},{9,8},{10,9},{11,10},{13,12},{... | collective-permute-start | bytes 1208 | tf_op jit(solution)/shard_map/ppermute | solution.py:25
Sparse Core Ops, SparseCore 0:
  339.4 31.8 all-reduce.11
where the time goes:
time: 382 us; the launch traced here: 380 us
  blocking collectives  176 us (46%)
  starting transfers between devices  72.7 us (19%)
  waiting for transfers between devices  42 us (11%)
  other arithmetic  34 us (9%)
  between operations  27.8 us (7%)
  local copies, waits for them, and re-layouts  18.5 us (5%)
  matrix products  8.41 us (2%)
    psum x4, blocking collectives, paired_totals(): lax.psum((jnp.sum(residual * residual), jnp.sum(residual * image)), ('til...  176 us
    ppermute x12, starting transfers between devices, extended(): lax.ppermute(tail, axis, [(i, (i + 1) % count) for i in range(ends)])  44.9 us
    psum x1, waiting for transfers between devices, body(): totals = lax.psum(partial_sums, 'lev')  31.1 us
    ppermute x12, starting transfers between devices, extended(): lax.ppermute(head, axis, [((i + 1) % count, i) for i in range(ends)])  15.7 us
    reduce_sum x4, other arithmetic, paired_totals(): jnp.sum(residual * image)  14 us
  transfers between devices with their start and end apart: 27, of which 7 were waited for; matrix products, arithmetic and copies ran while one was open for 11% of the time, Pallas kernels for 0%

commit v1 on v0

--- a/solution.py
+++ b/solution.py
@@ -71,7 +71,9 @@
 
 
 def paired_totals(residual, image):
-    return lax.psum((jnp.sum(residual * residual), jnp.sum(residual * image)), ("tiles", "lev"))
+    return lax.psum(
+        lax.psum((jnp.sum(residual * residual), jnp.sum(residual * image)), "lev"), "tiles"
+    )
 
 
 def krylov_merged(faces, rhs, start):

time: 382 us -> 324 us (0.85)
  blocking collectives: 176 us -> 127 us
  starting transfers between devices: 72.7 us -> 67.7 us
    psum x4 -> x8, blocking collectives: 176 us -> 127 us  [the longest x4 89.8 us: paired_totals(): lax.psum(lax.psum((jnp.sum(residual * residual), jnp.sum(residual * image...]
  transfers between devices with their start and end apart: 27 -> 27, of which waited for: 7 -> 6; matrix products, arithmetic and copies ran while one was open for 11% -> 13% of each run, Pallas kernels for 0% -> 0%
where the time goes in v1:
time: 324 us; the launch traced here: 322 us
  blocking collectives  127 us (39%)
  starting transfers between devices  67.7 us (21%)
  waiting for transfers between devices  38.3 us (12%)
  other arithmetic  34 us (10%)
  between operations  28 us (9%)
  local copies, waits for them, and re-layouts  18.4 us (6%)
  matrix products  8.41 us (3%)
    psum x4, blocking collectives, paired_totals(): lax.psum(lax.psum((jnp.sum(residual * residual), jnp.sum(residual * image...  89.8 us
    ppermute x12, starting transfers between devices, extended(): lax.ppermute(tail, axis, [(i, (i + 1) % count) for i in range(ends)])  44.1 us
    psum x4, blocking collectives, paired_totals(): lax.psum((jnp.sum(residual * residual), jnp.sum(residual * image)), 'lev')  37.4 us
    psum x1, waiting for transfers between devices, body(): totals = lax.psum(partial_sums, 'lev')  28.3 us
    ppermute x12, starting transfers between devices, extended(): lax.ppermute(head, axis, [((i + 1) % count, i) for i in range(ends)])  15.7 us
    reduce_sum x4, other arithmetic, paired_totals(): jnp.sum(residual * image)  13.9 us
    concatenate x6, local copies, waits for them, and re-layouts, extended(): jnp.concatenate([lax.ppermute(tail, axis, [(i, (i + 1) % count) for i in...  7.39 us
  transfers between devices with their start and end apart: 27, of which 6 were waited for; matrix products, arithmetic and copies ran while one was open for 13% of the time, Pallas kernels for 0%

profile of v1, /device:TPU:0, one launch (start us, length us, event | category | flops | bytes accessed | tf_op | source)
XLA Modules:
  0.0 322.0 jit_solution(923926127803403673)
XLA Ops:
  8.3 1.3 collective-permute-start
  9.6 5.5 %collective-permute-start.1 = (f32[10,1,1024]{2,1,0:T(1,128)S(1)}, f32[10,1,1024]{2,1,0:T(1,128)S(1)}, u32[]{:S(2)}, u32[]{:S(2)}) collective-permute-start(f32[10,1,1024]{2,1,0:T(1,128)S(1)} %get-tuple-element.54), channel_id=1, source_target_pairs={{0,4},{4,8},{8,12},{12,16},{16,20},{20,24},{24,28},{1,5},{5,9},{9,... | collective-permute-start | bytes 122888 | tf_op jit(solution)/shard_map/ppermute | solution.py:23
  15.2 1.6 collective-permute-done.1
  18.0 1.3 collective-permute-start.2
  19.3 3.0 collective-permute-start.3
  22.3 1.4 add_multiply_fusion
  24.5 2.2 power_multiply_fusion
  26.8 1.3 collective-permute-start.4
  28.1 5.4 %collective-permute-start.5 = (f32[10,1,1024]{2,1,0:T(1,128)S(1)}, f32[10,1,1024]{2,1,0:T(1,128)S(1)}, u32[]{:S(2)}, u32[]{:S(2)}) collective-permute-start(f32[10,1,1024]{2,1,0:T(1,128)S(1)} %get-tuple-element.52), channel_id=1, source_target_pairs={{0,4},{4,8},{8,12},{12,16},{16,20},{20,24},{24,28},{1,5},{5,9},{9,... | collective-permute-start | bytes 122888 | tf_op jit(solution)/shard_map/ppermute | solution.py:23
  35.9 1.3 collective-permute-start.6
  37.2 3.0 collective-permute-start.7
  42.0 3.4 %fusion.11 = (f32[10,8,1024]{2,1,0:T(8,128)S(1)}, f32[10,8,1024]{2,1,0:T(8,128)S(1)}, f32[10,8,1024]{2,1,0:T(8,128)S(1)}) fusion(f32[10,10,1026]{2,1,0:T(8,128)S(1)} %concatenate.125, f32[10,8,1024]{2,1,0:T(8,128)} %param.21, f32[10,8,1024]{2,1,0:T(8,128)} %param.20, f32[10,1,1024]{2,1,0:T(1,128)} %copy-done.9, f32[10,1,1024]{2,1,0:T(1,128)} %copy-done.10, ...), kind=kLoop, calls=%fused_computation.32 | loop fusion | flops 3686400 | bytes 3017856 | tf_op jit(solution)/shard_map/sub | solution.py:81
  45.5 1.3 collective-permute-start.8
  46.8 5.4 %collective-permute-start.9 = (f32[10,1,1024]{2,1,0:T(1,128)S(1)}, f32[10,1,1024]{2,1,0:T(1,128)S(1)}, u32[]{:S(2)}, u32[]{:S(2)}) collective-permute-start(f32[10,1,1024]{2,1,0:T(1,128)S(1)} %get-tuple-element.50), channel_id=1, source_target_pairs={{0,4},{4,8},{8,12},{12,16},{16,20},{20,24},{24,28},{1,5},{5,9},{9,... | collective-permute-start | bytes 122888 | tf_op jit(solution)/shard_map/ppermute | solution.py:23
  54.1 3.5 %collective-permute-start.10 = (f32[10,10,1]{2,1,0:T(8,128)S(1)}, f32[10,10,1]{2,1,0:T(8,128)S(1)}, u32[]{:S(2)}, u32[]{:S(2)}) collective-permute-start(f32[10,10,1]{2,1,0:T(8,128)S(1)} %get-tuple-element.39), channel_id=1, source_target_pairs={{0,1},{1,2},{2,3},{4,5},{5,6},{6,7},{8,9},{9,10},{10,11},{12,13},{... | collective-permute-start | bytes 1208 | tf_op jit(solution)/shard_map/ppermute | solution.py:23
  57.6 1.3 collective-permute-start.11
  59.7 3.8 %collective-permute-done.11 = f32[10,10,1]{2,1,0:T(8,128)S(1)} collective-permute-done((f32[10,10,1]{2,1,0:T(8,128)S(1)}, f32[10,10,1]{2,1,0:T(8,128)S(1)}, u32[]{:S(2)}, u32[]{:S(2)}) %collective-permute-start.11) | collective-permute-done | bytes 432 | tf_op jit(solution)/shard_map/ppermute | solution.py:25
  64.6 3.3 %multiply_reduce_fusion.5 = (f32[]{:T(128)}, f32[]{:T(128)}, f32[10,8,1024]{2,1,0:T(8,128)S(1)}) fusion(f32[10,8,1024]{2,1,0:T(8,128)S(1)} %get-tuple-element.29, f32[10,1,1024]{2,1,0:T(1,128)S(1)} %collective-permute-done.8, f32[10,1,1024]{2,1,0:T(1,128)S(1)} %collective-permute-done.9, f32[10,10,1]{2,1,0:T(8,128)S(1)} %collective-permute-done.10, ...), kind=kLoop, calls=%fused_computation.149 | loop fusion | flops 3522558 | bytes 2247016 | tf_op jit(solution)/shard_map/reduce_sum | solution.py:75
  68.0 9.3 %all-reduce.13 = (f32[]{:T(128)}, f32[]{:T(128)}) all-reduce(f32[]{:T(128)} %get-tuple-element.7, f32[]{:T(128)} %get-tuple-element.6), channel_id=1, replica_groups=mesh['tiles'=8,'lev'=4] {'lev'}, use_global_device_ids=true, to_apply=%region_4.5 | all-reduce | flops 2 | bytes 16 | tf_op jit(solution)/shard_map/psum | solution.py:75
  77.3 25.4 %all-reduce.9 = (f32[]{:T(128)}, f32[]{:T(128)}) all-reduce(f32[]{:T(128)} %get-tuple-element.22, f32[]{:T(128)} %get-tuple-element.23), channel_id=1, replica_groups=mesh['tiles'=8,'lev'=4] {'tiles'}, use_global_device_ids=true, to_apply=%region_5.6 | all-reduce | flops 2 | bytes 16 | tf_op jit(solution)/shard_map/psum | solution.py:74
  104.1 1.3 collective-permute-start.12
  105.4 4.5 %collective-permute-start.13 = (f32[10,1,1024]{2,1,0:T(1,128)S(1)}, f32[10,1,1024]{2,1,0:T(1,128)S(1)}, u32[]{:S(2)}, u32[]{:S(2)}) collective-permute-start(f32[10,1,1024]{2,1,0:T(1,128)S(1)} %get-tuple-element.48), channel_id=1, source_target_pairs={{0,4},{4,8},{8,12},{12,16},{16,20},{20,24},{24,28},{1,5},{5,9},{9,... | collective-permute-start | bytes 122888 | tf_op jit(solution)/shard_map/ppermute | solution.py:23
  110.6 3.8 %all-to-all-start = ((s32[8,1,8]{2,1,0:T(1,128)}), s32[8,1,8]{2,1,0:T(1,128)}, u32[]{:S(2)}, u32[]{:S(2)}) async-start(s32[8,1,8]{2,1,0:T(1,128)} %bitcast), calls=%async_computation | async-start | bytes 8192 | tf_op jit(solution)/shard_map/all_to_all | solution.py:148
  114.7 1.3 collective-permute-start.14
  118.5 2.5 collective-permute-done.15
  122.2 3.3 %multiply_reduce_fusion.3 = (f32[]{:T(128)}, f32[]{:T(128)}, f32[10,8,1024]{2,1,0:T(8,128)S(1)}) fusion(f32[10,8,1024]{2,1,0:T(8,128)S(1)} %multiply_subtract_fusion.2, f32[10,1,1024]{2,1,0:T(1,128)S(1)} %collective-permute-done.12, f32[10,1,1024]{2,1,0:T(1,128)S(1)} %collective-permute-done.13, f32[10,10,1]{2,1,0:T(8,128)S(1)} %collective-permute-done.14, ...), kind=kLoop, calls=%fused_computation.146 | loop fusion | flops 3522558 | bytes 2247016 | tf_op jit(solution)/shard_map/reduce_sum | solution.py:75
  125.5 9.4 %all-reduce.12 = (f32[]{:T(128)}, f32[]{:T(128)}) all-reduce(f32[]{:T(128)} %get-tuple-element.5, f32[]{:T(128)} %get-tuple-element.4), channel_id=1, replica_groups=mesh['tiles'=8,'lev'=4] {'lev'}, use_global_device_ids=true, to_apply=%region_10.11 | all-reduce | flops 2 | bytes 16 | tf_op jit(solution)/shard_map/psum | solution.py:75
  134.9 22.4 %all-reduce.8 = (f32[]{:T(128)}, f32[]{:T(128)}) all-reduce(f32[]{:T(128)} %get-tuple-element.20, f32[]{:T(128)} %get-tuple-element.21), channel_id=1, replica_groups=mesh['tiles'=8,'lev'=4] {'tiles'}, use_global_device_ids=true, to_apply=%region_11.12 | all-reduce | flops 2 | bytes 16 | tf_op jit(solution)/shard_map/psum | solution.py:74
  163.2 4.5 %collective-permute-start.17 = (f32[10,1,1024]{2,1,0:T(1,128)S(1)}, f32[10,1,1024]{2,1,0:T(1,128)S(1)}, u32[]{:S(2)}, u32[]{:S(2)}) collective-permute-start(f32[10,1,1024]{2,1,0:T(1,128)S(1)} %get-tuple-element.46), channel_id=1, source_target_pairs={{0,4},{4,8},{8,12},{12,16},{16,20},{20,24},{24,28},{1,5},{5,9},{9,... | collective-permute-start | bytes 122888 | tf_op jit(solution)/shard_map/ppermute | solution.py:23
  171.8 1.3 collective-permute-start.18
  173.1 1.5 collective-permute-start.19
  174.6 5.2 %fusion.74 = f32[32,1,1024]{2,1,0:T(1,128)} fusion(bf16[32,128,1024]{2,1,0:T(8,128)(2,1)} %param.12, bf16[32,128,1]{1,0,2:T(8,128)(2,1)S(1)} %bitcast.19), kind=kOutput, calls=%fused_computation.159 | convolution fusion | flops 8388608 | bytes 8527872 | tf_op jit(solution)/shard_map/bl,blt->bt/dot_general | solution.py:126
  179.8 2.3 concatenate.141
  182.1 3.9 %multiply_reduce_fusion.1 = (f32[]{:T(128)}, f32[]{:T(128)}, f32[10,8,1024]{2,1,0:T(8,128)}) fusion(f32[10,8,1024]{2,1,0:T(8,128)S(1)} %multiply_subtract_fusion.1, f32[10,1,1024]{2,1,0:T(1,128)S(1)} %collective-permute-done.16, f32[10,1,1024]{2,1,0:T(1,128)S(1)} %collective-permute-done.17, f32[10,10,1]{2,1,0:T(8,128)S(1)} %collective-permute-done.18, ...), kind=kLoop, calls=%fused_computation.142 | loop fusion | flops 3522558 | bytes 2247016 | tf_op jit(solution)/shard_map/reduce_sum | solution.py:75
  186.0 9.3 %all-reduce.11 = (f32[]{:T(128)}, f32[]{:T(128)}) all-reduce(f32[]{:T(128)} %get-tuple-element.3, f32[]{:T(128)} %get-tuple-element.2), channel_id=1, replica_groups=mesh['tiles'=8,'lev'=4] {'lev'}, use_global_device_ids=true, to_apply=%region_16.17 | all-reduce | flops 2 | bytes 16 | tf_op jit(solution)/shard_map/psum | solution.py:75
  195.3 19.7 %all-reduce.7 = (f32[]{:T(128)}, f32[]{:T(128)}) all-reduce(f32[]{:T(128)} %get-tuple-element.18, f32[]{:T(128)} %get-tuple-element.19), channel_id=1, replica_groups=mesh['tiles'=8,'lev'=4] {'tiles'}, use_global_device_ids=true, to_apply=%region_17.18 | all-reduce | flops 2 | bytes 16 | tf_op jit(solution)/shard_map/psum | solution.py:74
  218.7 1.7 multiply_reduce_fusion
  221.8 4.5 %collective-permute-start.21 = (f32[10,1,1024]{2,1,0:T(1,128)S(1)}, f32[10,1,1024]{2,1,0:T(1,128)S(1)}, u32[]{:S(2)}, u32[]{:S(2)}) collective-permute-start(f32[10,1,1024]{2,1,0:T(1,128)S(1)} %get-tuple-element.44), channel_id=1, source_target_pairs={{0,4},{4,8},{8,12},{12,16},{16,20},{20,24},{24,28},{1,5},{5,9},{9,... | collective-permute-start | bytes 122888 | tf_op jit(solution)/shard_map/ppermute | solution.py:23
  226.4 2.0 convolution_bitcast_fusion
  229.7 4.1 %all-to-all-start.1 = ((f32[8,8,1024]{2,1,0:T(8,128)}), f32[8,8,1024]{2,1,0:T(8,128)}, u32[]{:S(2)}, u32[]{:S(2)}) async-start(f32[8,8,1024]{2,1,0:T(8,128)} %convolution_bitcast_fusion), calls=%async_computation.1 | async-start | bytes 524288 | tf_op jit(solution)/shard_map/all_to_all | solution.py:147
  234.5 1.9 collective-permute-start.22
  238.3 1.8 reduce.3
  241.4 2.1 concatenate.147
  243.5 3.3 %fusion.70 = f32[]{:T(128)} fusion(f32[10,8,1024]{2,1,0:T(8,128)S(1)} %get-tuple-element.25, f32[10,1,1024]{2,1,0:T(1,128)} %copy-done.11, f32[10,1,1024]{2,1,0:T(1,128)} %copy-done.12, f32[10,10,1]{2,1,0:T(8,128)} %collective-permute-done.22, f32[10,10,1]{2,1,0:T(8,128)} %collective-permute-done.23, f32[10,8,1024]{2,1,0:T(8,128)S(1)} %get-tuple-element.30, ...), kind=kLoop, calls=%fused_computation.153 | loop fusion | flops 3358719 | bytes 1919332 | tf_op jit(solution)/shard_map/reduce_sum | solution.py:75
  246.8 9.4 %all-reduce.10 = (f32[]{:T(128)}, f32[]{:T(128)}) all-reduce(f32[]{:T(128)} %get-tuple-element.24, f32[]{:T(128)} %fusion.70), channel_id=1, replica_groups=mesh['tiles'=8,'lev'=4] {'lev'}, use_global_device_ids=true, to_apply=%region_22.23 | all-reduce | flops 2 | bytes 16 | tf_op jit(solution)/shard_map/psum | solution.py:75
  256.2 22.3 %all-reduce.6 = (f32[]{:T(128)}, f32[]{:T(128)}) all-reduce(f32[]{:T(128)} %get-tuple-element.16, f32[]{:T(128)} %get-tuple-element.17), channel_id=1, replica_groups=mesh['tiles'=8,'lev'=4] {'tiles'}, use_global_device_ids=true, to_apply=%region_23.24 | all-reduce | flops 2 | bytes 16 | tf_op jit(solution)/shard_map/psum | solution.py:74
  285.2 28.3 %all-reduce.16.cloned.1.call-done = f32[8,4096]{1,0:T(8,128)} async-done(((f32[8,4096]{1,0:T(8,128)}), f32[8,4096]{1,0:T(8,128)}) %all-reduce.16.cloned.1.call-update) | async-done | bytes 131088 | tf_op jit(solution)/shard_map/psum | solution.py:159
  313.5 1.6 copy.29
  (100 shorter events, 30.4 us)
Async XLA Ops:
  8.3 6.8 %collective-permute-start = (f32[10,1,1024]{2,1,0:T(1,128)S(1)}, f32[10,1,1024]{2,1,0:T(1,128)S(1)}, u32[]{:S(2)}, u32[]{:S(2)}) collective-permute-start(f32[10,1,1024]{2,1,0:T(1,128)S(1)} %get-tuple-element.55), channel_id=1, source_target_pairs={{4,0},{8,4},{12,8},{16,12},{20,16},{24,20},{28,24},{5,1},{9,5},{13... | collective-permute-start | bytes 122888 | tf_op jit(solution)/shard_map/ppermute | solution.py:25
  9.6 7.2 %collective-permute-start.1 = (f32[10,1,1024]{2,1,0:T(1,128)S(1)}, f32[10,1,1024]{2,1,0:T(1,128)S(1)}, u32[]{:S(2)}, u32[]{:S(2)}) collective-permute-start(f32[10,1,1024]{2,1,0:T(1,128)S(1)} %get-tuple-element.54), channel_id=1, source_target_pairs={{0,4},{4,8},{8,12},{12,16},{16,20},{20,24},{24,28},{1,5},{5,9},{9,... | collective-permute-start | bytes 122888 | tf_op jit(solution)/shard_map/ppermute | solution.py:23
  15.1 19.7 %copy-start.9 = (f32[10,1,1024]{2,1,0:T(1,128)}, f32[10,1,1024]{2,1,0:T(1,128)S(1)}, u32[]{:S(2)}) copy-start(f32[10,1,1024]{2,1,0:T(1,128)S(1)} %collective-permute-done) | copy-start | bytes 122884
  16.8 18.0 %copy-start.10 = (f32[10,1,1024]{2,1,0:T(1,128)}, f32[10,1,1024]{2,1,0:T(1,128)S(1)}, u32[]{:S(2)}) copy-start(f32[10,1,1024]{2,1,0:T(1,128)S(1)} %collective-permute-done.1) | copy-start | bytes 122884
  18.0 6.5 %collective-permute-start.2 = (f32[10,10,1]{2,1,0:T(8,128)S(1)}, f32[10,10,1]{2,1,0:T(8,128)S(1)}, u32[]{:S(2)}, u32[]{:S(2)}) collective-permute-start(f32[10,10,1]{2,1,0:T(8,128)S(1)} %get-tuple-element.42), channel_id=1, source_target_pairs={{1,0},{2,1},{3,2},{5,4},{6,5},{7,6},{9,8},{10,9},{11,10},{13,12},{... | collective-permute-start | bytes 1208 | tf_op jit(solution)/shard_map/ppermute | solution.py:25
  19.3 5.2 %collective-permute-start.3 = (f32[10,10,1]{2,1,0:T(8,128)S(1)}, f32[10,10,1]{2,1,0:T(8,128)S(1)}, u32[]{:S(2)}, u32[]{:S(2)}) collective-permute-start(f32[10,10,1]{2,1,0:T(8,128)S(1)} %get-tuple-element.43), channel_id=1, source_target_pairs={{0,1},{1,2},{2,3},{4,5},{5,6},{6,7},{8,9},{9,10},{10,11},{12,13},{... | collective-permute-start | bytes 1208 | tf_op jit(solution)/shard_map/ppermute | solution.py:23
  24.5 17.3 %copy-start.7 = (f32[10,10,1]{2,1,0:T(8,128)}, f32[10,10,1]{2,1,0:T(8,128)S(1)}, u32[]{:S(2)}) copy-start(f32[10,10,1]{2,1,0:T(8,128)S(1)} %collective-permute-done.2) | copy-start | bytes 1204
  24.5 17.3 %copy-start.8 = (f32[10,10,1]{2,1,0:T(8,128)}, f32[10,10,1]{2,1,0:T(8,128)S(1)}, u32[]{:S(2)}) copy-start(f32[10,10,1]{2,1,0:T(8,128)S(1)} %collective-permute-done.3) | copy-start | bytes 1204
  26.8 8.0 %collective-permute-start.4 = (f32[10,1,1024]{2,1,0:T(1,128)S(1)}, f32[10,1,1024]{2,1,0:T(1,128)S(1)}, u32[]{:S(2)}, u32[]{:S(2)}) collective-permute-start(f32[10,1,1024]{2,1,0:T(1,128)S(1)} %get-tuple-element.53), channel_id=1, source_target_pairs={{4,0},{8,4},{12,8},{16,12},{20,16},{24,20},{28,24},{5,1},{9,5},{13... | collective-permute-start | bytes 122888 | tf_op jit(solution)/shard_map/ppermute | solution.py:25
  28.1 7.6 %collective-permute-start.5 = (f32[10,1,1024]{2,1,0:T(1,128)S(1)}, f32[10,1,1024]{2,1,0:T(1,128)S(1)}, u32[]{:S(2)}, u32[]{:S(2)}) collective-permute-start(f32[10,1,1024]{2,1,0:T(1,128)S(1)} %get-tuple-element.52), channel_id=1, source_target_pairs={{0,4},{4,8},{8,12},{12,16},{16,20},{20,24},{24,28},{1,5},{5,9},{9,... | collective-permute-start | bytes 122888 | tf_op jit(solution)/shard_map/ppermute | solution.py:23
  34.8 6.6 %copy-start.14 = (s32[32]{0:T(128)}, s32[32]{0:T(128)S(1)}, u32[]{:S(2)}) copy-start(s32[32]{0:T(128)S(1)} %get-tuple-element.59) | copy-start | bytes 388
  34.8 5.4 %copy-start.3 = (f32[10,1,1024]{2,1,0:T(1,128)}, f32[10,1,1024]{2,1,0:T(1,128)S(1)}, u32[]{:S(2)}) copy-start(f32[10,1,1024]{2,1,0:T(1,128)S(1)} %collective-permute-done.4) | copy-start | bytes 122884
  35.7 4.6 %copy-start.5 = (f32[10,1,1024]{2,1,0:T(1,128)}, f32[10,1,1024]{2,1,0:T(1,128)S(1)}, u32[]{:S(2)}) copy-start(f32[10,1,1024]{2,1,0:T(1,128)S(1)} %collective-permute-done.5) | copy-start | bytes 122884
  35.9 5.5 %collective-permute-start.6 = (f32[10,10,1]{2,1,0:T(8,128)S(1)}, f32[10,10,1]{2,1,0:T(8,128)S(1)}, u32[]{:S(2)}, u32[]{:S(2)}) collective-permute-start(f32[10,10,1]{2,1,0:T(8,128)S(1)} %get-tuple-element.41), channel_id=1, source_target_pairs={{1,0},{2,1},{3,2},{5,4},{6,5},{7,6},{9,8},{10,9},{11,10},{13,12},{... | collective-permute-start | bytes 1208 | tf_op jit(solution)/shard_map/ppermute | solution.py:25
  37.2 4.2 %collective-permute-start.7 = (f32[10,10,1]{2,1,0:T(8,128)S(1)}, f32[10,10,1]{2,1,0:T(8,128)S(1)}, u32[]{:S(2)}, u32[]{:S(2)}) collective-permute-start(f32[10,10,1]{2,1,0:T(8,128)S(1)} %get-tuple-element.40), channel_id=1, source_target_pairs={{0,1},{1,2},{2,3},{4,5},{5,6},{6,7},{8,9},{9,10},{10,11},{12,13},{... | collective-permute-start | bytes 1208 | tf_op jit(solution)/shard_map/ppermute | solution.py:23
  41.4 0.7 copy-start.1
  45.4 76.8 %copy-start.2 = (f32[10,10,1]{2,1,0:T(8,128)S(1)}, f32[10,10,1]{2,1,0:T(8,128)}, u32[]{:S(2)}) copy-start(f32[10,10,1]{2,1,0:T(8,128)} %copy-done.1) | copy-start | bytes 1204
  45.4 76.7 %copy-start.4 = (f32[10,1,1024]{2,1,0:T(1,128)S(1)}, f32[10,1,1024]{2,1,0:T(1,128)}, u32[]{:S(2)}) copy-start(f32[10,1,1024]{2,1,0:T(1,128)} %copy-done.3) | copy-start | bytes 122884
  45.4 76.7 %copy-start.6 = (f32[10,1,1024]{2,1,0:T(1,128)S(1)}, f32[10,1,1024]{2,1,0:T(1,128)}, u32[]{:S(2)}) copy-start(f32[10,1,1024]{2,1,0:T(1,128)} %copy-done.5) | copy-start | bytes 122884
  45.5 7.4 %collective-permute-start.8 = (f32[10,1,1024]{2,1,0:T(1,128)S(1)}, f32[10,1,1024]{2,1,0:T(1,128)S(1)}, u32[]{:S(2)}, u32[]{:S(2)}) collective-permute-start(f32[10,1,1024]{2,1,0:T(1,128)S(1)} %get-tuple-element.51), channel_id=1, source_target_pairs={{4,0},{8,4},{12,8},{16,12},{20,16},{24,20},{28,24},{5,1},{9,5},{13... | collective-permute-start | bytes 122888 | tf_op jit(solution)/shard_map/ppermute | solution.py:25
  46.8 7.1 %collective-permute-start.9 = (f32[10,1,1024]{2,1,0:T(1,128)S(1)}, f32[10,1,1024]{2,1,0:T(1,128)S(1)}, u32[]{:S(2)}, u32[]{:S(2)}) collective-permute-start(f32[10,1,1024]{2,1,0:T(1,128)S(1)} %get-tuple-element.50), channel_id=1, source_target_pairs={{0,4},{4,8},{8,12},{12,16},{16,20},{20,24},{24,28},{1,5},{5,9},{9,... | collective-permute-start | bytes 122888 | tf_op jit(solution)/shard_map/ppermute | solution.py:23
  52.9 61.6 %copy-start.13 = (s32[32]{0:T(128)}, s32[32]{0:T(128)S(1)}, u32[]{:S(2)}) copy-start(s32[32]{0:T(128)S(1)} %multiply_add_fusion.2) | copy-start | bytes 388
  54.1 5.5 %collective-permute-start.10 = (f32[10,10,1]{2,1,0:T(8,128)S(1)}, f32[10,10,1]{2,1,0:T(8,128)S(1)}, u32[]{:S(2)}, u32[]{:S(2)}) collective-permute-start(f32[10,10,1]{2,1,0:T(8,128)S(1)} %get-tuple-element.39), channel_id=1, source_target_pairs={{0,1},{1,2},{2,3},{4,5},{5,6},{6,7},{8,9},{9,10},{10,11},{12,13},{... | collective-permute-start | bytes 1208 | tf_op jit(solution)/shard_map/ppermute | solution.py:23
  57.6 5.9 %collective-permute-start.11 = (f32[10,10,1]{2,1,0:T(8,128)S(1)}, f32[10,10,1]{2,1,0:T(8,128)S(1)}, u32[]{:S(2)}, u32[]{:S(2)}) collective-permute-start(f32[10,10,1]{2,1,0:T(8,128)S(1)} %get-tuple-element.38), channel_id=1, source_target_pairs={{1,0},{2,1},{3,2},{5,4},{6,5},{7,6},{9,8},{10,9},{11,10},{13,12},{... | collective-permute-start | bytes 1208 | tf_op jit(solution)/shard_map/ppermute | solution.py:25
  104.1 10.4 %collective-permute-start.12 = (f32[10,1,1024]{2,1,0:T(1,128)S(1)}, f32[10,1,1024]{2,1,0:T(1,128)S(1)}, u32[]{:S(2)}, u32[]{:S(2)}) collective-permute-start(f32[10,1,1024]{2,1,0:T(1,128)S(1)} %get-tuple-element.49), channel_id=1, source_target_pairs={{4,0},{8,4},{12,8},{16,12},{20,16},{24,20},{28,24},{5,1},{9,5},{13... | collective-permute-start | bytes 122888 | tf_op jit(solution)/shard_map/ppermute | solution.py:25
  105.4 9.1 %collective-permute-start.13 = (f32[10,1,1024]{2,1,0:T(1,128)S(1)}, f32[10,1,1024]{2,1,0:T(1,128)S(1)}, u32[]{:S(2)}, u32[]{:S(2)}) collective-permute-start(f32[10,1,1024]{2,1,0:T(1,128)S(1)} %get-tuple-element.48), channel_id=1, source_target_pairs={{0,4},{4,8},{8,12},{12,16},{16,20},{20,24},{24,28},{1,5},{5,9},{9,... | collective-permute-start | bytes 122888 | tf_op jit(solution)/shard_map/ppermute | solution.py:23
  110.6 119.1 %all-to-all-start = ((s32[8,1,8]{2,1,0:T(1,128)}), s32[8,1,8]{2,1,0:T(1,128)}, u32[]{:S(2)}, u32[]{:S(2)}) async-start(s32[8,1,8]{2,1,0:T(1,128)} %bitcast), calls=%async_computation | async-start | bytes 8192 | tf_op jit(solution)/shard_map/all_to_all | solution.py:148
  114.7 3.8 %collective-permute-start.14 = (f32[10,10,1]{2,1,0:T(8,128)S(1)}, f32[10,10,1]{2,1,0:T(8,128)S(1)}, u32[]{:S(2)}, u32[]{:S(2)}) collective-permute-start(f32[10,10,1]{2,1,0:T(8,128)S(1)} %get-tuple-element.37), channel_id=1, source_target_pairs={{0,1},{1,2},{2,3},{4,5},{5,6},{6,7},{8,9},{9,10},{10,11},{12,13},{... | collective-permute-start | bytes 1208 | tf_op jit(solution)/shard_map/ppermute | solution.py:23
  116.0 5.0 %collective-permute-start.15 = (f32[10,10,1]{2,1,0:T(8,128)S(1)}, f32[10,10,1]{2,1,0:T(8,128)S(1)}, u32[]{:S(2)}, u32[]{:S(2)}) collective-permute-start(f32[10,10,1]{2,1,0:T(8,128)S(1)} %get-tuple-element.36), channel_id=1, source_target_pairs={{1,0},{2,1},{3,2},{5,4},{6,5},{7,6},{9,8},{10,9},{11,10},{13,12},{... | collective-permute-start | bytes 1208 | tf_op jit(solution)/shard_map/ppermute | solution.py:25
  161.9 7.9 %collective-permute-start.16 = (f32[10,1,1024]{2,1,0:T(1,128)S(1)}, f32[10,1,1024]{2,1,0:T(1,128)S(1)}, u32[]{:S(2)}, u32[]{:S(2)}) collective-permute-start(f32[10,1,1024]{2,1,0:T(1,128)S(1)} %get-tuple-element.47), channel_id=1, source_target_pairs={{4,0},{8,4},{12,8},{16,12},{20,16},{24,20},{28,24},{5,1},{9,5},{13... | collective-permute-start | bytes 122888 | tf_op jit(solution)/shard_map/ppermute | solution.py:25
  163.2 6.6 %collective-permute-start.17 = (f32[10,1,1024]{2,1,0:T(1,128)S(1)}, f32[10,1,1024]{2,1,0:T(1,128)S(1)}, u32[]{:S(2)}, u32[]{:S(2)}) collective-permute-start(f32[10,1,1024]{2,1,0:T(1,128)S(1)} %get-tuple-element.46), channel_id=1, source_target_pairs={{0,4},{4,8},{8,12},{12,16},{16,20},{20,24},{24,28},{1,5},{5,9},{9,... | collective-permute-start | bytes 122888 | tf_op jit(solution)/shard_map/ppermute | solution.py:23
  171.8 8.0 %collective-permute-start.18 = (f32[10,10,1]{2,1,0:T(8,128)S(1)}, f32[10,10,1]{2,1,0:T(8,128)S(1)}, u32[]{:S(2)}, u32[]{:S(2)}) collective-permute-start(f32[10,10,1]{2,1,0:T(8,128)S(1)} %get-tuple-element.35), channel_id=1, source_target_pairs={{0,1},{1,2},{2,3},{4,5},{5,6},{6,7},{8,9},{9,10},{10,11},{12,13},{... | collective-permute-start | bytes 1208 | tf_op jit(solution)/shard_map/ppermute | solution.py:23
  173.1 6.7 %collective-permute-start.19 = (f32[10,10,1]{2,1,0:T(8,128)S(1)}, f32[10,10,1]{2,1,0:T(8,128)S(1)}, u32[]{:S(2)}, u32[]{:S(2)}) collective-permute-start(f32[10,10,1]{2,1,0:T(8,128)S(1)} %get-tuple-element.34), channel_id=1, source_target_pairs={{1,0},{2,1},{3,2},{5,4},{6,5},{7,6},{9,8},{10,9},{11,10},{13,12},{... | collective-permute-start | bytes 1208 | tf_op jit(solution)/shard_map/ppermute | solution.py:25
  179.8 104.5 %copy-start = (f32[10,8,1024]{2,1,0:T(8,128)S(1)}, f32[10,8,1024]{2,1,0:T(8,128)}, u32[]{:S(2)}) copy-start(f32[10,8,1024]{2,1,0:T(8,128)} %param.21) | copy-start | bytes 983044
  220.5 7.9 %collective-permute-start.20 = (f32[10,1,1024]{2,1,0:T(1,128)S(1)}, f32[10,1,1024]{2,1,0:T(1,128)S(1)}, u32[]{:S(2)}, u32[]{:S(2)}) collective-permute-start(f32[10,1,1024]{2,1,0:T(1,128)S(1)} %get-tuple-element.45), channel_id=1, source_target_pairs={{4,0},{8,4},{12,8},{16,12},{20,16},{24,20},{28,24},{5,1},{9,5},{13... | collective-permute-start | bytes 122888 | tf_op jit(solution)/shard_map/ppermute | solution.py:25
  221.8 6.6 %collective-permute-start.21 = (f32[10,1,1024]{2,1,0:T(1,128)S(1)}, f32[10,1,1024]{2,1,0:T(1,128)S(1)}, u32[]{:S(2)}, u32[]{:S(2)}) collective-permute-start(f32[10,1,1024]{2,1,0:T(1,128)S(1)} %get-tuple-element.44), channel_id=1, source_target_pairs={{0,4},{4,8},{8,12},{12,16},{16,20},{20,24},{24,28},{1,5},{5,9},{9,... | collective-permute-start | bytes 122888 | tf_op jit(solution)/shard_map/ppermute | solution.py:23
  228.4 0.6 copy-start.11
  229.0 0.6 copy-start.12
  229.7 52.7 %all-to-all-start.1 = ((f32[8,8,1024]{2,1,0:T(8,128)}), f32[8,8,1024]{2,1,0:T(8,128)}, u32[]{:S(2)}, u32[]{:S(2)}) async-start(f32[8,8,1024]{2,1,0:T(8,128)} %convolution_bitcast_fusion), calls=%async_computation.1 | async-start | bytes 524288 | tf_op jit(solution)/shard_map/all_to_all | solution.py:147
  233.8 79.8 %all-reduce.16.cloned.1.call-start = ((), (), s32[]{:S(2)}) async-start(), calls=%async_computation.2 | async-start | bytes 262144 | tf_op jit(solution)/shard_map/psum | solution.py:159
  234.5 6.8 %collective-permute-start.22 = (f32[10,10,1]{2,1,0:T(8,128)}, f32[10,10,1]{2,1,0:T(8,128)}, u32[]{:S(2)}, u32[]{:S(2)}) collective-permute-start(f32[10,10,1]{2,1,0:T(8,128)} %get-tuple-element.33), channel_id=1, source_target_pairs={{0,1},{1,2},{2,3},{4,5},{5,6},{6,7},{8,9},{9,10},{10,11},{12,13},{... | collective-permute-start | bytes 1208 | tf_op jit(solution)/shard_map/ppermute | solution.py:23
  236.5 4.9 %collective-permute-start.23 = (f32[10,10,1]{2,1,0:T(8,128)}, f32[10,10,1]{2,1,0:T(8,128)}, u32[]{:S(2)}, u32[]{:S(2)}) collective-permute-start(f32[10,10,1]{2,1,0:T(8,128)} %get-tuple-element.32), channel_id=1, source_target_pairs={{1,0},{2,1},{3,2},{5,4},{6,5},{7,6},{9,8},{10,9},{11,10},{13,12},{... | collective-permute-start | bytes 1208 | tf_op jit(solution)/shard_map/ppermute | solution.py:25
Sparse Core Ops, SparseCore 0:
  284.4 29.0 all-reduce.15
